TPU v7x, 512 devices: a whole 4x8x8 slice. The times are simulated.
512 devices in a mesh: space: 32 (over y_lo, z), chaos: 16 (over x, y_hi, core).
Axes of the slice: x: 4, y: 8 (y_hi: 2, y_lo: 4; y = y_hi * 4 + y_lo), z: 8, core: 2. Of those that a mesh axis runs over, the one named last changes fastest.
Arguments:
- load_vectors: bfloat16 [256, 2, 16, 12288], P('chaos', None, None, 'space'), may hold values from -6 to 6
- stiff_tiles: bfloat16 [128, 3, 8, 2, 96, 96], P('space'), may hold values from -0.09375 to 0.09375
- tile_columns: int32 [128, 3], P('space'), may hold values from 0 to 5, as said below
- chaos_index: int32 [8, 256, 32], replicated, may hold values from 0 to 255, as said below
- chaos_value: bfloat16 [8, 256, 32], replicated, may hold values from -1 to 1
Outputs:
- response: float32 [256, 2, 16, 12288], P('chaos', None, None, 'space')
Inputs may be any that keep to these rules, and one draw needn't show every extreme that they name: `tile_columns`: in row b of one subdomain with local index l = b % 4, the three numbers are l + 1, one of 0 to l, and one of l + 2 to 5. `chaos_index`: for every k and i the 32 numbers are distinct and the first is i.
All inputs are finite; a program needn't handle non-finite values.
Results may differ from a plain program's by a relative error of at most 0.0029.
Values may be sent and summed in bfloat16 or wider, within the bound.
A program may use at most 128 MiB of HBM per device.

v0:
```python
import jax
import jax.numpy as jnp
from jax import lax
from jax.sharding import PartitionSpec as P

TILE = 96
NKL = 8
P_SIZE = 256


def with_halo(cells, sides, width):
    for axis, dim in sides:
        count = lax.axis_size(axis)
        ends = count - 1
        head = lax.slice_in_dim(cells, 0, width, axis=dim)
        tail = lax.slice_in_dim(cells, cells.shape[dim] - width, cells.shape[dim], axis=dim)
        cells = jnp.concatenate(
            [
                lax.ppermute(tail, axis, [(i, (i + 1) % count) for i in range(ends)]),
                cells,
                lax.ppermute(head, axis, [((i + 1) % count, i) for i in range(ends)]),
            ],
            axis=dim,
        )
    return cells


def dense_coupling(chaos_index, chaos_value):
    columns = jnp.arange(P_SIZE, dtype=jnp.int32)

    def one_term(index_pair):
        row_index, row_value = index_pair
        matches = row_index[:, :, None] == columns[None, None, :]
        summed = jnp.where(matches, row_value[:, :, None], jnp.zeros((), jnp.bfloat16)).sum(axis=1)
        return summed

    return lax.map(one_term, (chaos_index, chaos_value))


def body(load_vectors, stiff_tiles, tile_columns, chaos_index, chaos_value):
    extended = with_halo(load_vectors, (("space", 3),), TILE)
    own_terms = load_vectors.shape[0]
    blocks = stiff_tiles.shape[0]
    first_term = lax.axis_index("chaos") * own_terms
    own_index = lax.dynamic_slice_in_dim(chaos_index, first_term, own_terms, 1)
    own_value = lax.dynamic_slice_in_dim(chaos_value, first_term, own_terms, 1)
    coupling = dense_coupling(own_index, own_value)
    coupled_field = jnp.einsum(
        "kij,jcre->kicre",
        coupling,
        lax.all_gather(extended, "chaos", axis=0, tiled=True),
        preferred_element_type=jnp.float32,
    ).astype(jnp.bfloat16)
    terms = coupled_field.shape[1]
    cases = coupled_field.shape[3]
    coupled_field = coupled_field.reshape(NKL, terms, 2, cases, blocks + 2, TILE)
    real_part = stiff_tiles[:, :, :, 0]
    imag_part = stiff_tiles[:, :, :, 1]
    upper_row = jnp.stack([real_part, -imag_part], axis=3)
    lower_row = jnp.stack([imag_part, real_part], axis=3)
    complex_tiles = jnp.stack([upper_row, lower_row], axis=3)
    accum_sum = jnp.zeros((terms, 2, cases, blocks, TILE), jnp.float32)
    for tile_slot in range(stiff_tiles.shape[1]):
        columns = jnp.take(coupled_field, tile_columns[:, tile_slot], axis=4)
        accum_sum = accum_sum + jnp.einsum(
            "bkcdxy,kidrby->icrbx",
            complex_tiles[:, tile_slot],
            columns,
            preferred_element_type=jnp.float32,
        )
    result = accum_sum.reshape(terms, 2, cases, blocks * TILE)
    return result


def solution(mesh):
    in_specs = (
        P("chaos", None, None, "space"),
        P("space", None, None, None, None, None),
        P("space", None),
        P(),
        P(),
    )
    out_specs = P("chaos", None, None, "space")
    return jax.shard_map(body, mesh=mesh, in_specs=in_specs, out_specs=out_specs, check_vma=False)
```

profile of v0, /device:TPU:9, one launch (start us, length us, event | category | flops | bytes accessed | tf_op | source)
XLA Modules:
  0.0 222.4 jit_solution(17434653015442165927)
XLA Ops:
  6.5 0.0 copy-start
  6.5 0.0 all-gather.2.cloned.1.call-start
  6.5 1.2 copy.32
  7.7 0.1 fusion.59
  7.8 10.6 %collective-permute-start.1 = (bf16[16,2,16,96]{3,0,2,1:T(8,128)(2,1)S(1)}, bf16[16,2,16,96]{3,0,2,1:T(8,128)(2,1)S(1)}, u32[]{:S(2)}, u32[]{:S(2)}) collective-permute-start(bf16[16,2,16,96]{3,0,2,1:T(8,128)(2,1)S(1)} %get-tuple-element.96), channel_id=1, source_target_pairs={{16,0},{32,16},{48,32},{64,48},{80,64},{96,80},{112,96},{128,112},... | collective-permute-start | bytes 294920 | tf_op jit(solution)/shard_map/ppermute | solution.py:21
  18.4 1.9 collective-permute-start
  20.3 0.2 collective-permute-done.1
  20.5 5.7 %collective-permute-done = bf16[16,2,16,96]{3,0,2,1:T(8,128)(2,1)S(1)} collective-permute-done((bf16[16,2,16,96]{3,0,2,1:T(8,128)(2,1)S(1)}, bf16[16,2,16,96]{3,0,2,1:T(8,128)(2,1)S(1)}, u32[]{:S(2)}, u32[]{:S(2)}) %collective-permute-start) | collective-permute-done | bytes 98336 | tf_op jit(solution)/shard_map/ppermute | solution.py:19
  26.2 1.2 pad_maximum_fusion.2
  27.4 0.0 all-gather.2.cloned.1.call-update
  27.4 0.0 copy-done
  27.4 0.1 constant_dynamic-slice_fusion.1
  27.5 0.1 copy.64
  27.6 0.9 constant_dynamic-slice_fusion
  28.6 0.1 copy.65
  28.7 1.0 slice_reduce_fusion
  29.8 3.3 %fusion.58 = (bf16[4,3,8,1,96,96]{5,4,3,2,1,0:T(8,128)(2,1)S(1)}, bf16[4,3,8,1,96,96]{5,4,3,2,1,0:T(8,128)(2,1)S(1)}) fusion(bf16[4,3,8,2,96,96]{5,4,3,2,1,0:T(8,128)(2,1)} %param.10), kind=kLoop, calls=%fused_computation.62 | loop fusion | bytes 7077888 | tf_op jit(solution)/shard_map/slice | solution.py:57
  33.0 0.3 copy_negate_fusion
  33.3 5.0 %maximum_bitcast_fusion = (bf16[4,3,8,1,2,96,96]{6,5,2,4,3,0,1:T(8,128)(2,1)}, bf16[4,3,8,1,2,96,96]{6,5,2,4,3,0,1:T(8,128)(2,1)}) fusion(bf16[4,3,8,1,96,96]{5,4,2,3,0,1:T(8,128)(2,1)S(1)} %copy_negate_fusion, bf16[4,3,8,1,96,96]{5,4,3,2,1,0:T(8,128)(2,1)S(1)} %get-tuple-element.93, bf16[4,3,8,1,96,96]{5,4,3,2,1,0:T(8,128)(2,1)S(1)} %get-tuple-element.94), kind=kLoop, calls=%fused_computation.16 | loop fusion | flops 8847360 | bytes 12386304 | tf_op jit(solution)/shard_map/stack | solution.py:61
  38.4 2.4 %while.13 = (s32[]{:T(128)}, bf16[8,16,256]{2,1,0:T(8,128)(2,1)S(1)}, s32[8,16,32]{2,1,0:T(8,128)S(1)}, bf16[8,16,32]{2,1,0:T(8,128)(2,1)S(1)}, s32[]{:T(128)}) while((s32[]{:T(128)}, bf16[8,16,256]{2,1,0:T(8,128)(2,1)S(1)}, s32[8,16,32]{2,1,0:T(8,128)S(1)}, bf16[8,16,32]{2,1,0:T(8,128)(2,1)S(1)}, s32[]{:T(128)}) %tuple.37), condition=%wide.region_2.3_spmd.clone, body=%wide.region_0.2_spmd.clone.sunk | while | flops 389122 | bytes 33873 | solution.py:37
  38.4 0.2 fusion.62
  38.7 0.2 fusion.62
  39.0 0.2 fusion.62
  39.3 0.2 fusion.62
  39.6 0.2 fusion.62
  39.9 0.2 fusion.62
  40.2 0.2 fusion.62
  40.5 0.2 fusion.62
  40.8 113.3 %all-gather.2.cloned.1.call-done = bf16[256,2,16,576]{3,0,2,1:T(8,128)(2,1)} async-done(((bf16[16,2,16,576]{3,0,2,1:T(8,128)(2,1)}), bf16[256,2,16,576]{3,0,2,1:T(8,128)(2,1)}) %all-gather.2.cloned.1.call-update) | async-done | bytes 9437200 | tf_op jit(solution)/shard_map/all_gather | solution.py:51
  154.0 7.9 %fusion.21 = bf16[8,16,2,16,576]{4,1,3,2,0:T(8,128)(2,1)} fusion(bf16[256,2,16,576]{3,0,2,1:T(8,128)(2,1)} %all-gather.2.cloned.1.call-done, bf16[8,16,256]{2,1,0:T(8,128)(2,1)S(1)} %get-tuple-element.71), kind=kOutput, calls=%fused_computation.35 | convolution fusion | flops 1210318848 | bytes 14221312 | tf_op jit(solution)/shard_map/kij,jcre->kicre/dot_general | solution.py:48
  161.9 13.6 %reshape.62 = bf16[8,16,2,16,6,96]{5,4,1,3,2,0:T(8,128)(2,1)} reshape(bf16[8,16,2,16,576]{4,1,3,2,0:T(8,128)(2,1)} %fusion.21) | data formatting | bytes 9437184 | tf_op jit(solution)/shard_map/reshape | solution.py:56
  175.5 10.1 %copy.36 = bf16[8,16,2,16,6,96]{5,3,2,1,0,4:T(8,128)(2,1)} copy(bf16[8,16,2,16,6,96]{5,4,1,3,2,0:T(8,128)(2,1)} %reshape.62) | data formatting | bytes 9437184 | tf_op jit(solution)/shard_map/reshape | solution.py:56
  185.7 5.8 %gather_fusion = bf16[4,8,16,2,16,96]{5,4,3,2,1,0:T(8,128)(2,1)} fusion(bf16[8,16,2,16,6,96]{5,3,2,1,0,4:T(8,128)(2,1)} %copy.36, s32[1024]{0:T(1024)S(1)} %pad_clamp_fusion.2), kind=kCustom, calls=%fused_computation.clone | custom fusion | bytes 6291472 | tf_op jit(solution)/shard_map/jit(_take)/gather | solution.py:64
  191.5 5.8 %gather_fusion.1 = bf16[4,8,16,2,16,96]{5,4,3,2,1,0:T(8,128)(2,1)} fusion(bf16[8,16,2,16,6,96]{5,3,2,1,0,4:T(8,128)(2,1)} %copy.36, s32[1024]{0:T(1024)S(1)} %pad_clamp_fusion.1), kind=kCustom, calls=%fused_computation.1.clone | custom fusion | bytes 6291472 | tf_op jit(solution)/shard_map/jit(_take)/gather | solution.py:64
  197.3 0.0 slice-start
  197.3 5.9 %gather_fusion.2 = bf16[4,8,16,2,16,96]{5,4,3,2,1,0:T(8,128)(2,1)} fusion(bf16[8,16,2,16,6,96]{5,3,2,1,0,4:T(8,128)(2,1)} %copy.36, s32[1024]{0:T(1024)S(1)} %pad_clamp_fusion), kind=kCustom, calls=%fused_computation.2.clone | custom fusion | bytes 6291472 | tf_op jit(solution)/shard_map/jit(_take)/gather | solution.py:64
  203.2 0.0 slice-start.1
  203.2 0.0 copy-start.3
  203.2 0.0 slice-start.2
  203.2 4.6 %fusion.24 = f32[4,16,16,2,96]{4,2,3,1,0:T(8,128)S(1)} fusion(bf16[4,3,8,1,2,96,96]{6,5,2,4,3,0,1:T(8,128)(2,1)} %get-tuple-element.101, bf16[4,3,8,1,2,96,96]{6,5,2,4,3,0,1:T(8,128)(2,1)} %get-tuple-element.102, bf16[4,8,16,2,16,96]{5,4,3,2,1,0:T(8,128)(2,1)} %gather_fusion, pred[4]{0:T(512)(128)(4,1)S(1)} %compare_and_fusion.2), kind=kOutput, calls=%fused_computation.37 | convolution fusion | flops 610271232 | bytes 11010052 | tf_op jit(solution)/shard_map/bkcdxy,kidrby->icrbx/dot_general | solution.py:65
  207.8 0.0 slice-done
  207.8 0.0 slice-done.1
  207.8 1.0 copy-done.3
  208.8 0.0 slice-start.3
  208.8 0.0 copy-start.2
  208.8 3.1 %fusion.49 = f32[4,16,16,2,96]{4,2,3,1,0:T(8,128)S(1)} fusion(f32[4,16,16,2,96]{4,2,3,1,0:T(8,128)S(1)} %fusion.24, bf16[4,3,8,1,2,96,96]{6,5,2,4,3,0,1:T(8,128)(2,1)S(1)} %bitcast.101, bf16[4,3,8,1,2,96,96]{6,5,2,4,3,0,1:T(8,128)(2,1)} %get-tuple-element.102, bf16[4,8,16,2,16,96]{5,4,3,2,1,0:T(8,128)(2,1)S(1)} %copy-done.3, ...), kind=kOutput, calls=%fused_computation.42 | convolution fusion | flops 610467840 | bytes 11796484 | tf_op jit(solution)/shard_map/bkcdxy,kidrby->icrbx/dot_general | solution.py:65
  212.0 0.0 slice-done.2
  212.0 0.0 slice-done.3
  212.0 0.1 copy-done.2
  212.1 0.0 copy-start.1
  212.1 1.4 fusion.44
  213.4 0.7 copy.45
  214.2 1.4 reshape.17
  215.5 0.0 copy-done.1
  (34 shorter events, 0.2 us)
Async XLA Ops:
  6.5 20.9 %copy-start = (s32[8,256,32]{1,2,0:T(8,128)S(1)}, s32[8,256,32]{1,2,0:T(8,128)}, u32[]{:S(2)}) copy-start(s32[8,256,32]{1,2,0:T(8,128)} %param.12) | copy-start | bytes 786436
  6.5 147.5 %all-gather.2.cloned.1.call-start = ((), (), s32[]{:S(2)}) async-start(), calls=%async_computation | async-start | bytes 11141120 | tf_op jit(solution)/shard_map/all_gather | solution.py:51
  7.8 12.7 %collective-permute-start.1 = (bf16[16,2,16,96]{3,0,2,1:T(8,128)(2,1)S(1)}, bf16[16,2,16,96]{3,0,2,1:T(8,128)(2,1)S(1)}, u32[]{:S(2)}, u32[]{:S(2)}) collective-permute-start(bf16[16,2,16,96]{3,0,2,1:T(8,128)(2,1)S(1)} %get-tuple-element.96), channel_id=1, source_target_pairs={{16,0},{32,16},{48,32},{64,48},{80,64},{96,80},{112,96},{128,112},... | collective-permute-start | bytes 294920 | tf_op jit(solution)/shard_map/ppermute | solution.py:21
  18.4 7.8 %collective-permute-start = (bf16[16,2,16,96]{3,0,2,1:T(8,128)(2,1)S(1)}, bf16[16,2,16,96]{3,0,2,1:T(8,128)(2,1)S(1)}, u32[]{:S(2)}, u32[]{:S(2)}) collective-permute-start(bf16[16,2,16,96]{3,0,2,1:T(8,128)(2,1)S(1)} %get-tuple-element.95), channel_id=1, source_target_pairs={{0,16},{16,32},{32,48},{48,64},{64,80},{80,96},{96,112},{112,128},... | collective-permute-start | bytes 294920 | tf_op jit(solution)/shard_map/ppermute | solution.py:19
  197.3 10.5 %slice-start = ((s8[4718592]{0:T(1024)(128)(4,1)}), s8[524288]{0:T(1024)(128)(4,1)S(1)}, s32[]{:S(2)}) async-start(s8[4718592]{0:T(1024)(128)(4,1)} %bitcast.100), calls=%async_computation.1 | async-start | bytes 1048576
  203.2 4.6 %slice-start.1 = ((s8[4718592]{0:T(1024)(128)(4,1)}), s8[4194304]{0:T(1024)(128)(4,1)S(1)}, s32[]{:S(2)}) async-start(s8[4718592]{0:T(1024)(128)(4,1)} %bitcast.100), calls=%async_computation.2 | async-start | bytes 8388608
  203.2 5.6 %copy-start.3 = (bf16[4,8,16,2,16,96]{5,4,3,2,1,0:T(8,128)(2,1)S(1)}, bf16[4,8,16,2,16,96]{5,4,3,2,1,0:T(8,128)(2,1)}, u32[]{:S(2)}) copy-start(bf16[4,8,16,2,16,96]{5,4,3,2,1,0:T(8,128)(2,1)} %gather_fusion.1) | copy-start | bytes 9437188
  203.2 8.8 %slice-start.2 = ((s8[4718592]{0:T(1024)(128)(4,1)}), s8[4194304]{0:T(1024)(128)(4,1)S(1)}, s32[]{:S(2)}) async-start(s8[4718592]{0:T(1024)(128)(4,1)} %bitcast.102), calls=%async_computation.3 | async-start | bytes 8388608
  208.8 3.1 %slice-start.3 = ((s8[4718592]{0:T(1024)(128)(4,1)}), s8[524288]{0:T(1024)(128)(4,1)S(1)}, s32[]{:S(2)}) async-start(s8[4718592]{0:T(1024)(128)(4,1)} %bitcast.102), calls=%async_computation.4 | async-start | bytes 1048576
  208.8 3.2 %copy-start.2 = (bf16[4,8,16,2,16,96]{5,4,3,2,1,0:T(8,128)(2,1)S(1)}, bf16[4,8,16,2,16,96]{5,4,3,2,1,0:T(8,128)(2,1)}, u32[]{:S(2)}) copy-start(bf16[4,8,16,2,16,96]{5,4,3,2,1,0:T(8,128)(2,1)} %gather_fusion.2) | copy-start | bytes 9437188
  212.1 3.5 %copy-start.1 = (s32[8,256,32]{1,2,0:T(8,128)S(1)}, s32[8,256,32]{1,2,0:T(8,128)}, u32[]{:S(2)}) copy-start(s32[8,256,32]{1,2,0:T(8,128)} %param.12) | copy-start | bytes 786436
Sparse Core Ops, SparseCore 0:
  27.5 126.4 all-gather.1
where the time goes:
time: 223 us; the launch traced here: 222 us
  waiting for transfers between devices  119 us (53%)
  local copies, waits for them, and re-layouts  51.5 us (23%)
  matrix products  16.9 us (8%)
  between operations  13.6 us (6%)
  starting transfers between devices  12.5 us (6%)
  other arithmetic  8.46 us (4%)
    all_gather x1, waiting for transfers between devices, body(): lax.all_gather(extended, 'chaos', axis=0, tiled=True)  113 us
    reshape x2, local copies, waits for them, and re-layouts, body(): coupled_field.reshape(NKL, terms, 2, cases, blocks + 2, TILE)  23.7 us
    gather x3, local copies, waits for them, and re-layouts, body(): columns = jnp.take(coupled_field, tile_columns[:, tile_slot], axis=4)  17.5 us
    ppermute x1, starting transfers between devices, with_halo(): lax.ppermute(head, axis, [((i + 1) % count, i) for i in range(ends)])  10.6 us
    dot_general x3, matrix products, body(): jnp.einsum('bkcdxy,kidrby->icrbx', complex_tiles[:, tile_slot], columns,...  9.03 us
    dot_general x1, matrix products, body(): jnp.einsum('kij,jcre->kicre', coupling, lax.all_gather(extended, 'chaos',...  7.9 us
    ppermute x1, waiting for transfers between devices, with_halo(): lax.ppermute(tail, axis, [(i, (i + 1) % count) for i in range(ends)])  5.66 us
    another operation x1, other arithmetic, body(): complex_tiles = jnp.stack([upper_row, lower_row], axis=3)  5.02 us
  transfers between devices with their start and end apart: 3, of which 3 were waited for; matrix products, arithmetic and copies ran while one was open for 6% of the time, Pallas kernels for 0%

commit v1 on v0

--- a/solution.py
+++ b/solution.py
@@ -6,6 +6,13 @@
 TILE = 96
 NKL = 8
 P_SIZE = 256
+
+
+def gather_over(array, axis, dim):
+    peers = lax.axis_size(axis)
+    parts = jnp.stack([array for _ in range(peers)])
+    parts = lax.all_to_all(parts, axis, split_axis=0, concat_axis=0)
+    return jnp.concatenate(parts, axis=dim)
 
 
 def with_halo(cells, sides, width):
@@ -48,7 +55,7 @@
     coupled_field = jnp.einsum(
         "kij,jcre->kicre",
         coupling,
-        lax.all_gather(extended, "chaos", axis=0, tiled=True),
+        gather_over(extended, "chaos", 0),
         preferred_element_type=jnp.float32,
     ).astype(jnp.bfloat16)
     terms = coupled_field.shape[1]

time: 223 us -> 349 us (1.57)
  the two profiles are of different devices: /device:TPU:9 before, /device:TPU:214 now
where the time goes in v1:
time: 349 us; the launch traced here: 348 us
  waiting for transfers between devices  235 us (67%)
  local copies, waits for them, and re-layouts  70.5 us (20%)
  matrix products  18.1 us (5%)
  starting transfers between devices  15.8 us (5%)
  other arithmetic  8.61 us (2%)
    all_to_all x1, waiting for transfers between devices, gather_over(): parts = lax.all_to_all(parts, axis, split_axis=0, concat_axis=0)  229 us
    reshape x2, local copies, waits for them, and re-layouts, body(): coupled_field.reshape(NKL, terms, 2, cases, blocks + 2, TILE)  23.6 us
    gather x3, local copies, waits for them, and re-layouts, body(): columns = jnp.take(coupled_field, tile_columns[:, tile_slot], axis=4)  17.8 us
    reshape x1, local copies, waits for them, and re-layouts, gather_over(): return jnp.concatenate(parts, axis=dim)  15.3 us
    dot_general x1, matrix products, body(): jnp.einsum('kij,jcre->kicre', coupling, gather_over(extended, 'chaos', 0)...  9.27 us
    dot_general x3, matrix products, body(): jnp.einsum('bkcdxy,kidrby->icrbx', complex_tiles[:, tile_slot], columns,...  8.81 us
    all_to_all x1, starting transfers between devices, gather_over(): parts = lax.all_to_all(parts, axis, split_axis=0, concat_axis=0)  8.39 us
  transfers between devices with their start and end apart: 3, of which 3 were waited for; matrix products, arithmetic and copies ran while one was open for 3% of the time, Pallas kernels for 0%

profile of v1, /device:TPU:214, one launch (start us, length us, event | category | flops | bytes accessed | tf_op | source)
XLA Modules:
  0.0 348.3 jit_solution(10360924640731632063)
XLA Ops:
  0.0 0.0 copy-start
  0.0 1.1 fusion.59
  1.1 5.5 %collective-permute-start = (bf16[16,2,16,96]{3,2,1,0:T(8,128)(2,1)S(1)}, bf16[16,2,16,96]{3,2,1,0:T(8,128)(2,1)S(1)}, u32[]{:S(2)}, u32[]{:S(2)}) collective-permute-start(bf16[16,2,16,96]{3,2,1,0:T(8,128)(2,1)S(1)} %get-tuple-element.95), channel_id=1, source_target_pairs={{0,16},{16,32},{32,48},{48,64},{64,80},{80,96},{96,112},{112,128},... | collective-permute-start | bytes 294920 | tf_op jit(solution)/shard_map/ppermute | solution.py:26
  6.6 1.9 collective-permute-start.1
  8.5 0.8 collective-permute-done
  9.4 5.3 %collective-permute-done.1 = bf16[16,2,16,96]{3,2,1,0:T(8,128)(2,1)S(1)} collective-permute-done((bf16[16,2,16,96]{3,2,1,0:T(8,128)(2,1)S(1)}, bf16[16,2,16,96]{3,2,1,0:T(8,128)(2,1)S(1)}, u32[]{:S(2)}, u32[]{:S(2)}) %collective-permute-start.1) | collective-permute-done | bytes 98336 | tf_op jit(solution)/shard_map/ppermute | solution.py:28
  14.7 1.4 pad_maximum_fusion.2
  16.0 5.2 %stack.12 = bf16[16,16,2,16,576]{4,3,2,1,0:T(8,128)(2,1)} broadcast(bf16[16,2,16,576]{3,2,1,0:T(8,128)(2,1)S(1)} %pad_maximum_fusion.2), dimensions={1,2,3,4} | broadcast | bytes 10027008 | tf_op jit(solution)/shard_map/stack | solution.py:13
  21.2 0.0 copy-start.4
  21.2 0.0 copy-start.5
  21.2 8.4 %all-to-all-start = ((bf16[16,16,2,16,576]{4,3,2,1,0:T(8,128)(2,1)}), bf16[16,16,2,16,576]{4,3,2,1,0:T(8,128)(2,1)}, u32[]{:S(2)}, u32[]{:S(2)}) async-start(bf16[16,16,2,16,576]{4,3,2,1,0:T(8,128)(2,1)} %stack.12), calls=%async_computation | async-start | bytes 20971520 | tf_op jit(solution)/shard_map/all_to_all | solution.py:14
  29.6 0.0 copy-done
  29.7 0.1 constant_dynamic-slice_fusion.1
  29.8 0.1 copy.58
  29.9 0.0 copy-done.4
  29.9 0.1 constant_dynamic-slice_fusion
  30.0 0.1 copy.59
  30.1 0.0 copy-done.5
  30.1 0.2 slice_reduce_fusion
  30.4 3.3 fusion.58
  33.6 0.3 copy_negate_fusion
  34.0 5.0 %maximum_bitcast_fusion = (bf16[4,3,8,1,2,96,96]{6,5,2,4,3,0,1:T(8,128)(2,1)}, bf16[4,3,8,1,2,96,96]{6,5,2,4,3,0,1:T(8,128)(2,1)}) fusion(bf16[4,3,8,1,96,96]{5,4,2,3,0,1:T(8,128)(2,1)S(1)} %copy_negate_fusion, bf16[4,3,8,1,96,96]{5,4,3,2,1,0:T(8,128)(2,1)S(1)} %get-tuple-element.93, bf16[4,3,8,1,96,96]{5,4,3,2,1,0:T(8,128)(2,1)S(1)} %get-tuple-element.94), kind=kLoop, calls=%fused_computation.16 | loop fusion | flops 8847360 | bytes 12386304 | tf_op jit(solution)/shard_map/stack | solution.py:68
  38.9 2.4 while.13
  39.0 0.2 fusion.62
  39.3 0.2 fusion.62
  39.6 0.2 fusion.62
  39.9 0.2 fusion.62
  40.2 0.2 fusion.62
  40.5 0.2 fusion.62
  40.8 0.2 fusion.62
  41.1 0.2 fusion.62
  41.4 228.6 %all-to-all-done = bf16[16,16,2,16,576]{4,3,2,1,0:T(8,128)(2,1)} async-done(((bf16[16,16,2,16,576]{4,3,2,1,0:T(8,128)(2,1)}), bf16[16,16,2,16,576]{4,3,2,1,0:T(8,128)(2,1)}, u32[]{:S(2)}, u32[]{:S(2)}) %all-to-all-start) | async-done | bytes 9437216 | tf_op jit(solution)/shard_map/all_to_all | solution.py:14
  270.0 15.3 %copy.28 = bf16[256,2,16,576]{0,3,2,1:T(8,128)(2,1)} copy(bf16[256,2,16,576]{3,2,1,0:T(8,128)(2,1)} %bitcast.2) | data formatting | bytes 18874368 | tf_op jit(solution)/shard_map/reshape | solution.py:15
  285.3 9.3 %fusion.21 = bf16[8,16,2,16,576]{4,1,3,2,0:T(8,128)(2,1)} fusion(bf16[256,2,16,576]{0,3,2,1:T(8,128)(2,1)} %copy.28, bf16[8,16,256]{2,1,0:T(8,128)(2,1)S(1)} %get-tuple-element.71), kind=kOutput, calls=%fused_computation.35 | convolution fusion | flops 1210318848 | bytes 14221312 | tf_op jit(solution)/shard_map/kij,jcre->kicre/dot_general | solution.py:55
  294.6 13.6 %reshape.68 = bf16[8,16,2,16,6,96]{5,4,1,3,2,0:T(8,128)(2,1)} reshape(bf16[8,16,2,16,576]{4,1,3,2,0:T(8,128)(2,1)} %fusion.21) | data formatting | bytes 9437184 | tf_op jit(solution)/shard_map/reshape | solution.py:63
  308.2 10.0 %copy.30 = bf16[8,16,2,16,6,96]{5,3,2,1,0,4:T(8,128)(2,1)} copy(bf16[8,16,2,16,6,96]{5,4,1,3,2,0:T(8,128)(2,1)} %reshape.68) | data formatting | bytes 9437184 | tf_op jit(solution)/shard_map/reshape | solution.py:63
  318.2 5.9 %gather_fusion = bf16[4,8,16,2,16,96]{5,4,3,2,1,0:T(8,128)(2,1)} fusion(bf16[8,16,2,16,6,96]{5,3,2,1,0,4:T(8,128)(2,1)} %copy.30, s32[1024]{0:T(1024)S(1)} %pad_clamp_fusion.2), kind=kCustom, calls=%fused_computation.clone | custom fusion | bytes 6291472 | tf_op jit(solution)/shard_map/jit(_take)/gather | solution.py:71
  324.1 5.9 %gather_fusion.1 = bf16[4,8,16,2,16,96]{5,4,3,2,1,0:T(8,128)(2,1)} fusion(bf16[8,16,2,16,6,96]{5,3,2,1,0,4:T(8,128)(2,1)} %copy.30, s32[1024]{0:T(1024)S(1)} %pad_clamp_fusion.1), kind=kCustom, calls=%fused_computation.1.clone | custom fusion | bytes 6291472 | tf_op jit(solution)/shard_map/jit(_take)/gather | solution.py:71
  329.9 0.0 slice-start
  329.9 6.0 %gather_fusion.2 = bf16[4,8,16,2,16,96]{5,4,3,2,1,0:T(8,128)(2,1)} fusion(bf16[8,16,2,16,6,96]{5,3,2,1,0,4:T(8,128)(2,1)} %copy.30, s32[1024]{0:T(1024)S(1)} %pad_clamp_fusion), kind=kCustom, calls=%fused_computation.2.clone | custom fusion | bytes 6291472 | tf_op jit(solution)/shard_map/jit(_take)/gather | solution.py:71
  336.0 0.0 slice-start.1
  336.0 0.0 copy-start.3
  336.0 0.0 slice-start.2
  336.0 4.6 %fusion.24 = f32[4,16,16,2,96]{4,2,3,1,0:T(8,128)S(1)} fusion(bf16[4,3,8,1,2,96,96]{6,5,2,4,3,0,1:T(8,128)(2,1)} %get-tuple-element.101, bf16[4,3,8,1,2,96,96]{6,5,2,4,3,0,1:T(8,128)(2,1)} %get-tuple-element.102, bf16[4,8,16,2,16,96]{5,4,3,2,1,0:T(8,128)(2,1)} %gather_fusion, pred[4]{0:T(512)(128)(4,1)S(1)} %compare_and_fusion.2), kind=kOutput, calls=%fused_computation.37 | convolution fusion | flops 610271232 | bytes 11010052 | tf_op jit(solution)/shard_map/bkcdxy,kidrby->icrbx/dot_general | solution.py:72
  340.5 0.0 slice-done
  340.6 0.0 slice-done.1
  340.6 1.0 copy-done.3
  341.6 0.0 slice-start.3
  341.6 0.0 copy-start.2
  341.6 2.9 fusion.49
  344.5 0.0 slice-done.2
  344.5 0.0 slice-done.3
  344.5 0.3 copy-done.2
  344.8 0.0 copy-start.1
  344.9 1.4 fusion.44
  346.2 0.7 copy.39
  346.9 1.4 reshape.23
  348.3 0.0 copy-done.1
  (34 shorter events, 0.2 us)
Async XLA Ops:
  0.0 29.6 %copy-start = (s32[8,256,32]{1,2,0:T(8,128)S(1)}, s32[8,256,32]{1,2,0:T(8,128)}, u32[]{:S(2)}) copy-start(s32[8,256,32]{1,2,0:T(8,128)} %param.12) | copy-start | bytes 786436
  1.1 8.2 %collective-permute-start = (bf16[16,2,16,96]{3,2,1,0:T(8,128)(2,1)S(1)}, bf16[16,2,16,96]{3,2,1,0:T(8,128)(2,1)S(1)}, u32[]{:S(2)}, u32[]{:S(2)}) collective-permute-start(bf16[16,2,16,96]{3,2,1,0:T(8,128)(2,1)S(1)} %get-tuple-element.95), channel_id=1, source_target_pairs={{0,16},{16,32},{32,48},{48,64},{64,80},{80,96},{96,112},{112,128},... | collective-permute-start | bytes 294920 | tf_op jit(solution)/shard_map/ppermute | solution.py:26
  6.6 8.1 %collective-permute-start.1 = (bf16[16,2,16,96]{3,2,1,0:T(8,128)(2,1)S(1)}, bf16[16,2,16,96]{3,2,1,0:T(8,128)(2,1)S(1)}, u32[]{:S(2)}, u32[]{:S(2)}) collective-permute-start(bf16[16,2,16,96]{3,2,1,0:T(8,128)(2,1)S(1)} %get-tuple-element.96), channel_id=1, source_target_pairs={{16,0},{32,16},{48,32},{64,48},{80,64},{96,80},{112,96},{128,112},... | collective-permute-start | bytes 294920 | tf_op jit(solution)/shard_map/ppermute | solution.py:28
  21.2 8.6 %copy-start.4 = (bf16[8,256,32]{1,2,0:T(8,128)(2,1)S(1)}, bf16[8,256,32]{1,2,0:T(8,128)(2,1)}, u32[]{:S(2)}) copy-start(bf16[8,256,32]{1,2,0:T(8,128)(2,1)} %param.13) | copy-start | bytes 393220
  21.2 8.8 %copy-start.5 = (s32[4,3]{1,0:T(4,128)S(1)}, s32[4,3]{1,0:T(4,128)}, u32[]{:S(2)}) copy-start(s32[4,3]{1,0:T(4,128)} %param.11) | copy-start | bytes 148
  21.2 248.7 %all-to-all-start = ((bf16[16,16,2,16,576]{4,3,2,1,0:T(8,128)(2,1)}), bf16[16,16,2,16,576]{4,3,2,1,0:T(8,128)(2,1)}, u32[]{:S(2)}, u32[]{:S(2)}) async-start(bf16[16,16,2,16,576]{4,3,2,1,0:T(8,128)(2,1)} %stack.12), calls=%async_computation | async-start | bytes 20971520 | tf_op jit(solution)/shard_map/all_to_all | solution.py:14
  329.9 10.6 %slice-start = ((s8[4718592]{0:T(1024)(128)(4,1)}), s8[524288]{0:T(1024)(128)(4,1)S(1)}, s32[]{:S(2)}) async-start(s8[4718592]{0:T(1024)(128)(4,1)} %bitcast.101), calls=%async_computation.1 | async-start | bytes 1048576
  336.0 4.6 %slice-start.1 = ((s8[4718592]{0:T(1024)(128)(4,1)}), s8[4194304]{0:T(1024)(128)(4,1)S(1)}, s32[]{:S(2)}) async-start(s8[4718592]{0:T(1024)(128)(4,1)} %bitcast.101), calls=%async_computation.2 | async-start | bytes 8388608
  336.0 5.6 %copy-start.3 = (bf16[4,8,16,2,16,96]{5,4,3,2,1,0:T(8,128)(2,1)S(1)}, bf16[4,8,16,2,16,96]{5,4,3,2,1,0:T(8,128)(2,1)}, u32[]{:S(2)}) copy-start(bf16[4,8,16,2,16,96]{5,4,3,2,1,0:T(8,128)(2,1)} %gather_fusion.1) | copy-start | bytes 9437188
  336.0 8.5 %slice-start.2 = ((s8[4718592]{0:T(1024)(128)(4,1)}), s8[4194304]{0:T(1024)(128)(4,1)S(1)}, s32[]{:S(2)}) async-start(s8[4718592]{0:T(1024)(128)(4,1)} %bitcast.103), calls=%async_computation.3 | async-start | bytes 8388608
  341.6 2.9 slice-start.3
  341.6 3.2 copy-start.2
  344.8 3.5 copy-start.1
